TPU v7x, 32 devices: a whole 2x2x4 slice. The times are simulated.
32 devices in a mesh: dp: 4 (over z), tensor: 8 (over y, x, core).
Axes of the slice: x: 2, y: 2, z: 4, core: 2. Of those that a mesh axis runs over, the one named last changes fastest.
Arguments:
- hidden_in: bfloat16 [4, 1024, 2304], P('dp', 'tensor'), may hold values from -6 to 6
- prompt_len: int32 [4], P('dp'), may hold values from 1 to 1024, 2560 in all
- start_pos: int32 [4], P('dp'), may hold values from 0 to 511
- routes: int32 [4, 1024, 2], P('dp'), may hold values from 0 to 7, as said below
- trainer_qkv: float32 [2304, 3, 2048], P(('tensor', 'dp')), may hold values from -1 to 1
- trainer_out: float32 [2048, 2304], P(('tensor', 'dp')), may hold values from -0.125 to 0.125
- trainer_gate: float32 [2304, 5760], P('tensor'), may hold values from -0.125 to 0.125
- trainer_up: float32 [2304, 5760], P('tensor'), may hold values from -0.125 to 0.125
- trainer_down: float32 [2304, 5760], P('tensor'), may hold values from -0.078125 to 0.078125
- attn_gain: float32 [2304], replicated, may hold values from 0.25 to 1.75
- moe_gain: float32 [2304], replicated, may hold values from 0.25 to 1.75
- router: bfloat16 [2304, 8], replicated, may hold values from -0.125 to 0.125
Outputs:
- server_qkv: bfloat16 [2304, 3, 2048], P(None, None, 'tensor')
- server_out: bfloat16 [2048, 2304], P('tensor')
- server_gate: bfloat16 [2304, 5760], P(None, 'tensor')
- server_up: bfloat16 [2304, 5760], P(None, 'tensor')
- server_down: bfloat16 [2304, 5760], P(None, 'tensor')
- hidden_out: bfloat16 [4, 1024, 2304], P('dp', 'tensor')
- kv_cache: bfloat16 [4, 2, 1024, 2048], P('dp', None, None, 'tensor')
Inputs may be any that keep to these rules, and one draw needn't show every extreme that they name: `routes`: each row names two different experts; expert 0 is named by at most 512 rows of each prompt and by exactly 512 rows of some prompt.
All inputs are finite; a program needn't handle non-finite values. No bound on the sum of `prompt_len` on one device may be relied on, other than what follows from the above.
Results may differ from a plain program's by a relative error of at most 0.011.
The roundings to bfloat16 on the way count: a program that leaves them out, or rounds other values in their place, can miss the bound.
Values may be sent and summed in bfloat16 or wider, within the bound.
No kernel may reach another device: no remote copies, remote signals or barrier semaphores. Data moves between devices by JAX's collectives and lax.ppermute only.
A program may use at most 256 MiB of HBM per device.

v0:
```python
import jax
import jax.numpy as jnp
from jax import lax
from jax.sharding import PartitionSpec as P

HEAD_DIM = 64


def rms_scale(values, gain_row):
    mean_sq = jnp.mean(values * values, axis=-1, keepdims=True)
    return values * lax.rsqrt(mean_sq + 1e-05) * gain_row


def rotate(head_block, positions):
    half_dim = head_block.shape[-1] // 2
    inv_freq = jnp.power(
        10000.0, jnp.arange(half_dim, dtype=jnp.float32) * (-2.0 / head_block.shape[-1])
    )
    angles = positions.astype(jnp.float32)[:, None] * inv_freq[None, :]
    cosine = jnp.cos(angles)[:, None, :]
    sine_part = jnp.sin(angles)[:, None, :]
    first_half = head_block[..., :half_dim]
    second_half = head_block[..., half_dim:]
    return jnp.concatenate(
        [
            first_half * cosine - second_half * sine_part,
            second_half * cosine + first_half * sine_part,
        ],
        axis=-1,
    )


def attend_block(query_blk, key_blk, value_blk, row_start):
    scores = jnp.einsum(
        "qhd,khd->hqk", query_blk, key_blk, preferred_element_type=jnp.float32
    ) * query_blk.shape[-1] ** (-0.5)
    row_ids = row_start + jnp.arange(query_blk.shape[0], dtype=jnp.int32)
    col_ids = jnp.arange(key_blk.shape[0], dtype=jnp.int32)
    scores = jnp.where(row_ids[None, :, None] >= col_ids[None, None, :], scores, -1e30)
    row_max = jnp.max(scores, axis=-1, keepdims=True)
    exp_scores = jnp.exp(scores - row_max)
    attn_probs = (exp_scores / jnp.sum(exp_scores, axis=-1, keepdims=True)).astype(jnp.bfloat16)
    return jnp.einsum(
        "hqk,khd->qhd", attn_probs, value_blk, preferred_element_type=jnp.float32
    ).astype(jnp.bfloat16)


def shards(
    hidden_in,
    prompt_len,
    start_pos,
    routes,
    trainer_qkv,
    trainer_out,
    trainer_gate,
    trainer_up,
    trainer_down,
    attn_gain,
    moe_gain,
    router,
):
    tensor_size = lax.axis_size("tensor")
    replica_count = lax.axis_size("dp")
    expert_mats = (
        lax.all_to_all(
            trainer_gate.astype(jnp.bfloat16), "tensor", split_axis=1, concat_axis=0, tiled=True
        ),
        lax.all_to_all(
            trainer_up.astype(jnp.bfloat16), "tensor", split_axis=1, concat_axis=0, tiled=True
        ),
        lax.all_to_all(
            trainer_down.astype(jnp.bfloat16), "tensor", split_axis=1, concat_axis=0, tiled=True
        ),
    )
    server_gate, server_up, server_down = expert_mats
    qkv_cast = trainer_qkv.astype(jnp.bfloat16)
    out_cast = trainer_out.astype(jnp.bfloat16)
    column_part = lax.all_to_all(qkv_cast, "tensor", split_axis=2, concat_axis=0, tiled=True)
    stacked, server_out = (
        lax.all_gather(column_part, "dp", axis=0, tiled=True),
        lax.all_gather(out_cast, "dp", axis=0, tiled=True),
    )
    block_rows = stacked.shape[0] // (replica_count * tensor_size)
    server_qkv = (
        stacked.reshape(replica_count, tensor_size, block_rows, 3, stacked.shape[2])
        .transpose(1, 0, 2, 3, 4)
        .reshape(stacked.shape)
    )
    rows_dev = hidden_in.shape[1]
    seq_len = rows_dev * tensor_size
    length = prompt_len[0]
    offset = start_pos[0]
    my_first = lax.axis_index("tensor") * rows_dev
    tokens = hidden_in[0].astype(jnp.float32)
    normed = rms_scale(tokens, attn_gain).astype(jnp.bfloat16)
    local_width = server_qkv.shape[2]
    heads_here = local_width // HEAD_DIM
    piece = lax.all_gather(normed, "tensor", axis=0, tiled=True)
    mixed = jnp.einsum("sd,dtc->stc", piece, server_qkv, preferred_element_type=jnp.float32)
    places = offset + jnp.arange(piece.shape[0], dtype=jnp.int32)
    query_rot = rotate(mixed[:, 0].reshape(-1, heads_here, HEAD_DIM), places).reshape(
        -1, local_width
    )
    key_rot = rotate(mixed[:, 1].reshape(-1, heads_here, HEAD_DIM), places).reshape(-1, local_width)
    qkv_rows = jnp.stack([query_rot, key_rot, mixed[:, 2]], axis=1).astype(jnp.bfloat16)
    query_all = qkv_rows[:, 0].reshape(seq_len, heads_here, HEAD_DIM)
    keys_all = qkv_rows[:, 1].reshape(seq_len, heads_here, HEAD_DIM)
    values_all = qkv_rows[:, 2].reshape(seq_len, heads_here, HEAD_DIM)
    block_len = min(512, seq_len)
    block_outs = []
    for block_id in range(seq_len // block_len):
        row_lo = block_id * block_len
        row_hi = row_lo + block_len
        query_blk = query_all[row_lo:row_hi]
        key_blk = keys_all[:row_hi]
        value_blk = values_all[:row_hi]
        block_result = attend_block(query_blk, key_blk, value_blk, row_lo)
        block_outs.append(block_result)
    attended = jnp.concatenate(block_outs, axis=0).reshape(seq_len, local_width)
    attn_sum = lax.psum_scatter(
        jnp.dot(attended, server_out, preferred_element_type=jnp.float32).astype(jnp.bfloat16),
        "tensor",
        scatter_dimension=0,
        tiled=True,
    ).astype(jnp.float32)
    middle = (tokens + attn_sum).astype(jnp.bfloat16)
    normed_moe = rms_scale(middle.astype(jnp.float32), moe_gain).astype(jnp.bfloat16)
    local_routes = lax.dynamic_slice_in_dim(routes[0], my_first, rows_dev, 0)
    local_valid = my_first + jnp.arange(rows_dev, dtype=jnp.int32) < length
    logits = jnp.dot(normed_moe, router, preferred_element_type=jnp.float32)
    expert_ids = jnp.arange(router.shape[1], dtype=jnp.int32)
    logit_first = jnp.sum(
        jnp.where(local_routes[:, 0:1] == expert_ids[None, :], logits, 0.0), axis=1
    )
    logit_second = jnp.sum(
        jnp.where(local_routes[:, 1:2] == expert_ids[None, :], logits, 0.0), axis=1
    )
    other_logit = jnp.where(local_routes[:, 0] == 0, logit_second, logit_first)
    local_routed = jnp.any(local_routes == 0, axis=1)
    route_w = jnp.where(local_routed, jax.nn.sigmoid(logits[:, 0] - other_logit), 0.0)
    gathered = lax.all_gather(normed_moe, "tensor", axis=0, tiled=True)
    seq_ids = jnp.arange(seq_len, dtype=jnp.int32)
    all_routed = jnp.any(routes[0] == 0, axis=1)
    capacity = seq_len // 2
    slot = jnp.cumsum(all_routed.astype(jnp.int32)) - 1
    slot_rows = (
        jnp.full((capacity,), seq_len, jnp.int32)
        .at[jnp.where(all_routed, slot, capacity)]
        .set(seq_ids, mode="drop")
    )
    picked = gathered[jnp.minimum(slot_rows, seq_len - 1)]
    gate_val = jnp.dot(picked, server_gate, preferred_element_type=jnp.float32)
    up_val = jnp.dot(picked, server_up, preferred_element_type=jnp.float32)
    act = (jax.nn.silu(gate_val) * up_val).astype(jnp.bfloat16)
    slot_sums = lax.dot_general(
        act, server_down, (((1,), (1,)), ((), ())), preferred_element_type=jnp.float32
    )
    terms = (
        jnp.zeros((seq_len, normed_moe.shape[1]), jnp.float32)
        .at[slot_rows]
        .add(slot_sums, mode="drop")
    )
    expert_sum = lax.psum_scatter(
        terms.astype(jnp.bfloat16), "tensor", scatter_dimension=0, tiled=True
    ).astype(jnp.float32)
    result = middle.astype(jnp.float32) + route_w[:, None] * expert_sum
    hidden_out = jnp.where(local_valid[:, None], result, 0.0).astype(jnp.bfloat16)[None]
    seq_valid = jnp.arange(seq_len, dtype=jnp.int32) < length
    cache_pair = jnp.where(
        seq_valid[None, :, None], qkv_rows[:, 1:3].transpose(1, 0, 2), jnp.zeros((), jnp.bfloat16)
    )
    return (
        server_qkv,
        server_out,
        server_gate,
        server_up,
        server_down,
        hidden_out,
        cache_pair[None],
    )


def solution(mesh):
    placed = (
        P("dp", "tensor", None),
        P("dp"),
        P("dp"),
        P("dp", None, None),
        P(("tensor", "dp"), None, None),
        P(("tensor", "dp"), None),
        P("tensor", None),
        P("tensor", None),
        P("tensor", None),
        P(),
        P(),
        P(),
    )
    return jax.shard_map(
        shards,
        mesh=mesh,
        in_specs=placed,
        out_specs=(
            P(None, None, "tensor"),
            P("tensor", None),
            P(None, "tensor"),
            P(None, "tensor"),
            P(None, "tensor"),
            P("dp", "tensor", None),
            P("dp", None, None, "tensor"),
        ),
        check_vma=False,
    )
```

profile of v0, /device:TPU:0, one launch (start us, length us, event | category | flops | bytes accessed | tf_op | source)
XLA Modules:
  0.0 508.5 jit_solution(11771919291552511364)
XLA Ops:
  7.2 2.5 convert_element_type.86
  9.7 2.9 copy.59
  12.6 3.7 reshape.272
  16.3 18.9 %all_to_all.75 = bf16[8,2,27648]{2,1,0:T(2,128)(2,1)} all-to-all(bf16[8,2,27648]{2,1,0:T(2,128)(2,1)} %reshape.272), channel_id=1, replica_groups=mesh['dp'=4,'tensor'=8] {'tensor'}, dimensions={0} | all-to-all | bytes 1769472 | tf_op jit(solution)/shard_map/all_to_all | solution.py:78
  35.2 4.5 reshape.273
  39.7 2.2 copy.75
  46.1 65.7 %all-gather.5.cloned.1.call-done = bf16[2304,3,256]{2,0,1:T(8,128)(2,1)} async-done(((bf16[576,3,256]{2,0,1:T(8,128)(2,1)}), bf16[2304,3,256]{2,0,1:T(8,128)(2,1)}) %all-gather.5.cloned.1.call-update) | async-done | bytes 3538960 | tf_op jit(solution)/shard_map/all_gather | solution.py:80
  111.8 4.2 copy.62
  115.9 35.8 %all-gather.9.cloned.1.call-done = bf16[1024,2304]{1,0:T(8,128)(2,1)} async-done(((bf16[128,2304]{1,0:T(8,128)(2,1)}), bf16[1024,2304]{1,0:T(8,128)(2,1)}) %all-gather.9.cloned.1.call-update) | async-done | bytes 4718608 | tf_op jit(solution)/shard_map/all_gather | solution.py:98
  151.8 6.8 %fusion.61 = (bf16[1024,3,256]{0,2,1:T(8,128)(2,1)S(1)}, f32[1024,3,256]{0,2,1:T(8,128)S(1)}) fusion(bf16[2304,3,256]{2,0,1:T(8,128)(2,1)} %bitcast.102, bf16[1024,2304]{1,0:T(8,128)(2,1)} %all-gather.9.cloned.1.call-done), kind=kOutput, calls=%fused_computation.108 | convolution fusion | flops 3624665088 | bytes 12976128 | tf_op jit(solution)/shard_map/sd,dtc->stc/dot_general | solution.py:99
  159.2 5.4 %fusion.62 = (f32[4,512]{1,0:T(4,128)S(1)}, f32[4,512,1024]{2,1,0:T(8,128)}) fusion(pred[512,1024]{1,0:T(8,128)(4,1)S(1)} %iota_compare_fusion, bf16[1024,4,32]{0,2,1:T(8,128)(2,1)S(1)} %get-tuple-element.52, bf16[1024,4,32]{0,2,1:T(8,128)(2,1)S(1)} %get-tuple-element.53, bf16[1024,4,32]{0,2,1:T(8,128)(2,1)S(1)} %get-tuple-element.49, ...), kind=kOutput, calls=%fused_computation.109 | convolution fusion | flops 278397952 | bytes 9969664 | tf_op jit(solution)/shard_map/sub | solution.py:41
  164.6 3.7 fusion.63
  168.2 2.9 fusion.28
  171.1 1.8 copy-done.13
  172.9 1.5 fusion.27
  174.5 10.0 %all-gather.7.cloned.1.call-done = bf16[256,2304]{1,0:T(8,128)(2,1)} async-done(((bf16[64,2304]{1,0:T(8,128)(2,1)}), bf16[256,2304]{1,0:T(8,128)(2,1)}) %all-gather.7.cloned.1.call-update) | async-done | bytes 1179664 | tf_op jit(solution)/shard_map/all_gather | solution.py:81
  184.4 4.8 convolution_convert_fusion
  189.9 52.6 %reduce-scatter.3.cloned.1.call-done = bf16[128,2304]{1,0:T(8,128)(2,1)} async-done(((bf16[1024,2304]{1,0:T(8,128)(2,1)}), bf16[128,2304]{1,0:T(8,128)(2,1)}) %reduce-scatter.3.cloned.1.call-update) | async-done | bytes 589840 | tf_op jit(solution)/shard_map/reduce_scatter | solution.py:120
  242.4 1.3 fusion.18
  243.8 2.1 fusion.20
  246.0 4.9 convert_element_type.88
  250.9 8.5 %all_to_all.59 = bf16[288,8,720]{2,1,0:T(8,128)(2,1)} reshape(bf16[288,5760]{1,0:T(8,128)(2,1)} %convert_element_type.88) | data formatting | bytes 6635520 | tf_op jit(solution)/shard_map/all_to_all | solution.py:65
  259.4 4.6 copy.63
  264.0 4.5 all-to-all-start.1
  268.4 5.0 convert_element_type.89
  273.4 8.5 %all_to_all.63 = bf16[288,8,720]{2,1,0:T(8,128)(2,1)} reshape(bf16[288,5760]{1,0:T(8,128)(2,1)} %convert_element_type.89) | data formatting | bytes 6635520 | tf_op jit(solution)/shard_map/all_to_all | solution.py:68
  281.9 4.4 copy.64
  286.4 35.8 %all-to-all-done.1 = bf16[288,8,720]{2,0,1:T(8,128)(2,1)} async-done(((bf16[288,8,720]{2,0,1:T(8,128)(2,1)}), bf16[288,8,720]{2,0,1:T(8,128)(2,1)}, u32[]{:S(2)}, u32[]{:S(2)}) %all-to-all-start.1) | async-done | bytes 3317792 | tf_op jit(solution)/shard_map/all_to_all | solution.py:65
  322.2 4.5 all-to-all-start.2
  326.7 4.9 convert_element_type.90
  331.6 8.4 %all_to_all.67 = bf16[288,8,720]{2,1,0:T(8,128)(2,1)} reshape(bf16[288,5760]{1,0:T(8,128)(2,1)} %convert_element_type.90) | data formatting | bytes 6635520 | tf_op jit(solution)/shard_map/all_to_all | solution.py:71
  340.1 4.6 copy.65
  344.6 24.2 %all-to-all-done.2 = bf16[288,8,720]{2,0,1:T(8,128)(2,1)} async-done(((bf16[288,8,720]{2,0,1:T(8,128)(2,1)}), bf16[288,8,720]{2,0,1:T(8,128)(2,1)}, u32[]{:S(2)}, u32[]{:S(2)}) %all-to-all-start.2) | async-done | bytes 3317792 | tf_op jit(solution)/shard_map/all_to_all | solution.py:68
  368.8 4.5 all-to-all-start.3
  374.0 4.5 scatter_custom_fusion
  378.5 7.8 %gather_fusion = bf16[512,2304]{1,0:T(8,128)(2,1)S(1)} fusion(bf16[1024,2304]{1,0:T(8,128)(2,1)} %all-gather.11.cloned.1.call-done, s32[1024]{0:T(1024)S(1)} %pad_clamp_fusion), kind=kCustom, calls=%fused_computation | custom fusion | bytes 4720640 | tf_op jit(solution)/shard_map/gather | solution.py:151
  386.4 5.0 fusion.72
  391.4 24.0 %all-to-all-done.3 = bf16[288,8,720]{2,0,1:T(8,128)(2,1)} async-done(((bf16[288,8,720]{2,0,1:T(8,128)(2,1)}), bf16[288,8,720]{2,0,1:T(8,128)(2,1)}, u32[]{:S(2)}, u32[]{:S(2)}) %all-to-all-start.3) | async-done | bytes 3317792 | tf_op jit(solution)/shard_map/all_to_all | solution.py:71
  415.4 9.9 %fusion.32 = f32[512,2304]{1,0:T(8,128)} fusion(bf16[2304,720]{1,0:T(8,128)(2,1)} %bitcast.12, f32[512,720]{0,1:T(8,128)} %fusion.72, bf16[512,2304]{1,0:T(8,128)(2,1)S(1)} %gather_fusion, bf16[2304,720]{1,0:T(8,128)(2,1)} %bitcast.10), kind=kOutput, calls=%fused_computation.51 | convolution fusion | flops 3399598080 | bytes 15187968 | tf_op jit(solution)/shard_map/dot_general | solution.py:155
  425.3 13.3 %scatter_custom_fusion.1 = f32[1024,2304]{1,0:T(8,128)} fusion(s32[512]{0:T(512)S(1)} %get-tuple-element.57, f32[512,2304]{1,0:T(8,128)} %fusion.32, f32[]{:T(128)} %constant.20.clone.1), kind=kCustom, calls=%fused_computation.12 | custom fusion | flops 1179648 | bytes 9437696 | tf_op jit(solution)/shard_map/scatter-add | solution.py:161
  438.6 6.4 %convert_element_type.109 = bf16[1024,2304]{1,0:T(8,128)(2,1)} convert(f32[1024,2304]{1,0:T(8,128)} %scatter_custom_fusion.1) | non-fusion elementwise | flops 2359296 | bytes 14155776 | tf_op jit(solution)/shard_map/convert_element_type | solution.py:164
  445.7 5.7 %copy.68 = bf16[2304,720]{0,1:T(8,128)(2,1)} copy(bf16[2304,720]{1,0:T(8,128)(2,1)} %bitcast.8) | data formatting | bytes 6635520
  451.4 5.9 %copy.69 = bf16[2304,720]{0,1:T(8,128)(2,1)} copy(bf16[2304,720]{1,0:T(8,128)(2,1)} %bitcast.10) | data formatting | bytes 6635520
  457.3 5.7 %copy.70 = bf16[2304,720]{0,1:T(8,128)(2,1)} copy(bf16[2304,720]{1,0:T(8,128)(2,1)} %bitcast.12) | data formatting | bytes 6635520
  463.2 1.1 fusion.29
  464.2 2.3 copy.71
  466.8 31.4 %reduce-scatter.5.cloned.1.call-done = bf16[128,2304]{1,0:T(8,128)(2,1)} async-done(((bf16[1024,2304]{1,0:T(8,128)(2,1)}), bf16[128,2304]{1,0:T(8,128)(2,1)}) %reduce-scatter.5.cloned.1.call-update) | async-done | bytes 589840 | tf_op jit(solution)/shard_map/reduce_scatter | solution.py:163
  498.2 2.2 fusion.33
  (75 shorter events, 6.8 us)
Async XLA Ops:
  7.2 459.3 %copy-start = (bf16[2304,8]{0,1:T(8,128)(2,1)S(1)}, bf16[2304,8]{0,1:T(8,128)(2,1)}, u32[]{:S(2)}) copy-start(bf16[2304,8]{0,1:T(8,128)(2,1)} %param.23) | copy-start | bytes 110596
  7.2 104.6 %all-gather.5.cloned.1.call-start = ((), (), s32[]{:S(2)}) async-start(), calls=%async_computation.6 | async-start | bytes 4423680 | tf_op jit(solution)/shard_map/all_gather | solution.py:80
  35.2 6.8 %copy-start.1 = (bf16[1,128,2304]{2,1,0:T(8,128)(2,1)S(1)}, bf16[1,128,2304]{2,1,0:T(8,128)(2,1)}, u32[]{:S(2)}) copy-start(bf16[1,128,2304]{2,1,0:T(8,128)(2,1)} %param.12) | copy-start | bytes 1769476
  35.2 7.0 %copy-start.10 = (f32[2304]{0:T(1024)S(1)}, f32[2304]{0:T(1024)}, u32[]{:S(2)}) copy-start(f32[2304]{0:T(1024)} %param.21) | copy-start | bytes 27652
  39.7 3.6 copy-start.9
  41.9 109.9 %all-gather.9.cloned.1.call-start = ((), (), s32[]{:S(2)}) async-start(), calls=%async_computation.8 | async-start | bytes 5308416 | tf_op jit(solution)/shard_map/all_gather | solution.py:98
  43.2 141.2 %all-gather.7.cloned.1.call-start = ((), (), s32[]{:S(2)}) async-start(), calls=%async_computation.7 | async-start | bytes 1474560 | tf_op jit(solution)/shard_map/all_gather | solution.py:81
  44.1 198.4 %reduce-scatter.3.cloned.1.call-start = ((), (), s32[]{:S(2)}) async-start(), calls=%async_computation.9 | async-start | bytes 5308416 | tf_op jit(solution)/shard_map/reduce_scatter | solution.py:120
  159.2 5.4 %copy-start.5 = (bf16[1024,4,32]{0,2,1:T(8,128)(2,1)}, bf16[1024,4,32]{0,2,1:T(8,128)(2,1)S(1)}, u32[]{:S(2)}) copy-start(bf16[1024,4,32]{0,2,1:T(8,128)(2,1)S(1)} %get-tuple-element.48) | copy-start | bytes 786436
  159.2 5.4 %copy-start.7 = (bf16[1024,4,32]{0,2,1:T(8,128)(2,1)}, bf16[1024,4,32]{0,2,1:T(8,128)(2,1)S(1)}, u32[]{:S(2)}) copy-start(bf16[1024,4,32]{0,2,1:T(8,128)(2,1)S(1)} %get-tuple-element.49) | copy-start | bytes 786436
  168.2 4.7 copy-start.13
  189.3 54.5 %copy-start.11 = (f32[2304]{0:T(1024)S(1)}, f32[2304]{0:T(1024)}, u32[]{:S(2)}) copy-start(f32[2304]{0:T(1024)} %param.22) | copy-start | bytes 27652
  189.3 189.2 %all-gather.11.cloned.1.call-start = ((), (), s32[]{:S(2)}) async-start(), calls=%async_computation.10 | async-start | bytes 5308416 | tf_op jit(solution)/shard_map/all_gather | solution.py:141
  264.0 58.2 %all-to-all-start.1 = ((bf16[288,8,720]{2,0,1:T(8,128)(2,1)}), bf16[288,8,720]{2,0,1:T(8,128)(2,1)}, u32[]{:S(2)}, u32[]{:S(2)}) async-start(bf16[288,8,720]{2,0,1:T(8,128)(2,1)} %copy.63), calls=%async_computation.1 | async-start | bytes 7077888 | tf_op jit(solution)/shard_map/all_to_all | solution.py:65
  322.2 46.6 %all-to-all-start.2 = ((bf16[288,8,720]{2,0,1:T(8,128)(2,1)}), bf16[288,8,720]{2,0,1:T(8,128)(2,1)}, u32[]{:S(2)}, u32[]{:S(2)}) async-start(bf16[288,8,720]{2,0,1:T(8,128)(2,1)} %copy.64), calls=%async_computation.2 | async-start | bytes 7077888 | tf_op jit(solution)/shard_map/all_to_all | solution.py:68
  344.6 28.7 %copy-start.12 = (s32[1,1024,2]{1,2,0:T(2,128)S(1)}, s32[1,1024,2]{1,2,0:T(2,128)}, u32[]{:S(2)}) copy-start(s32[1,1024,2]{1,2,0:T(2,128)} %param.15) | copy-start | bytes 24580
  368.8 46.6 %all-to-all-start.3 = ((bf16[288,8,720]{2,0,1:T(8,128)(2,1)}), bf16[288,8,720]{2,0,1:T(8,128)(2,1)}, u32[]{:S(2)}, u32[]{:S(2)}) async-start(bf16[288,8,720]{2,0,1:T(8,128)(2,1)} %copy.65), calls=%async_computation.3 | async-start | bytes 7077888 | tf_op jit(solution)/shard_map/all_to_all | solution.py:71
  373.3 124.9 %reduce-scatter.5.cloned.1.call-start = ((), (), s32[]{:S(2)}) async-start(), calls=%async_computation.11 | async-start | bytes 5308416 | tf_op jit(solution)/shard_map/reduce_scatter | solution.py:163
  457.3 5.7 %copy-start.6 = (bf16[1024,4,32]{0,2,1:T(8,128)(2,1)S(1)}, bf16[1024,4,32]{0,2,1:T(8,128)(2,1)}, u32[]{:S(2)}) copy-start(bf16[1024,4,32]{0,2,1:T(8,128)(2,1)} %copy-done.5) | copy-start | bytes 786436
  457.3 5.7 %copy-start.8 = (bf16[1024,4,32]{0,2,1:T(8,128)(2,1)S(1)}, bf16[1024,4,32]{0,2,1:T(8,128)(2,1)}, u32[]{:S(2)}) copy-start(bf16[1024,4,32]{0,2,1:T(8,128)(2,1)} %copy-done.7) | copy-start | bytes 786436
  463.1 3.4 copy-start.2
  463.1 35.1 %copy-start.3 = (bf16[128,2304]{1,0:T(8,128)(2,1)S(1)}, bf16[128,2304]{1,0:T(8,128)(2,1)}, u32[]{:S(2)}) copy-start(bf16[128,2304]{1,0:T(8,128)(2,1)} %reduce-scatter.3.cloned.1.call-done) | copy-start | bytes 1769476
  463.1 37.3 %copy-start.4 = (bf16[256,2304]{1,0:T(8,128)(2,1)S(1)}, bf16[256,2304]{1,0:T(8,128)(2,1)}, u32[]{:S(2)}) copy-start(bf16[256,2304]{1,0:T(8,128)(2,1)} %all-gather.7.cloned.1.call-done) | copy-start | bytes 3538948
Sparse Core Ops, SparseCore 0:
  42.0 69.6 all-gather.4
  114.2 37.5 all-gather.8
  153.9 30.4 all-gather.6
  189.4 52.9 reduce-scatter.2
  246.1 60.3 all-gather.10
  445.1 53.0 reduce-scatter.4
where the time goes:
time: 513 us; the launch traced here: 509 us
  waiting for transfers between devices  279 us (54%)
  local copies, waits for them, and re-layouts  91.6 us (18%)
  other arithmetic  47.8 us (9%)
  matrix products  40.3 us (8%)
  blocking collectives  18.9 us (4%)
  between operations  16 us (3%)
  starting transfers between devices  14.5 us (3%)
    all_gather x1, waiting for transfers between devices, shards(): lax.all_gather(column_part, 'dp', axis=0, tiled=True)  65.7 us
    reduce_scatter x1, waiting for transfers between devices, shards(): lax.psum_scatter(jnp.dot(attended, server_out, preferred_element_type=jnp...  52.6 us
    all_gather x1, waiting for transfers between devices, shards(): piece = lax.all_gather(normed, 'tensor', axis=0, tiled=True)  35.8 us
    all_to_all x1, waiting for transfers between devices, shards(): lax.all_to_all(trainer_gate.astype(jnp.bfloat16), 'tensor', split_axis=1,...  35.8 us
    reduce_scatter x1, waiting for transfers between devices, shards(): lax.psum_scatter(terms.astype(jnp.bfloat16), 'tensor', scatter_dimension=...  31.4 us
    unnamed x35, local copies, waits for them, and re-layouts  30.7 us
    all_to_all x1, waiting for transfers between devices, shards(): lax.all_to_all(trainer_up.astype(jnp.bfloat16), 'tensor', split_axis=1, c...  24.2 us
    all_to_all x1, waiting for transfers between devices, shards(): lax.all_to_all(trainer_down.astype(jnp.bfloat16), 'tensor', split_axis=1,...  24 us
  transfers between devices with their start and end apart: 9, of which 8 were waited for; matrix products, arithmetic and copies ran while one was open for 19% of the time, Pallas kernels for 0%

commit v1 on v0

--- a/solution.py
+++ b/solution.py
@@ -2,8 +2,15 @@
 import jax.numpy as jnp
 from jax import lax
 from jax.sharding import PartitionSpec as P
+from jax.lax import axis_index, axis_size, ppermute
 
 HEAD_DIM = 64
+
+
+def _trace_rings(tile_in, dimension_no):
+    prior = list(tile_in.shape[1:])
+    prior[dimension_no] *= tile_in.shape[0]
+    return jnp.moveaxis(tile_in, 0, dimension_no).reshape(prior)
 
 
 def rms_scale(values, gain_row):
@@ -95,7 +102,23 @@
     normed = rms_scale(tokens, attn_gain).astype(jnp.bfloat16)
     local_width = server_qkv.shape[2]
     heads_here = local_width // HEAD_DIM
-    piece = lax.all_gather(normed, "tensor", axis=0, tiled=True)
+    many = axis_size("tensor")
+    all_rows = [(to_i, (to_i + 1) % many) for to_i in range(many)]
+    fields = [(tick, i0) for i0, tick in all_rows]
+    built, shaped = ([], [])
+    for dd in range(many - 1):
+        if dd % 2 == 0:
+            after = ppermute(built[-1] if built else normed, axis_name="tensor", perm=all_rows)
+            built.append(after)
+        else:
+            f_next = ppermute(shaped[-1] if shaped else normed, axis_name="tensor", perm=fields)
+            shaped.append(f_next)
+    q_next = jnp.stack([*built[::-1], normed, *shaped])
+    out_arr = axis_index("tensor")
+    y = len(built)
+    part_now = out_arr - y
+    q_next = q_next[(jnp.arange(many) - part_now) % many]
+    piece = _trace_rings(q_next, 0)
     mixed = jnp.einsum("sd,dtc->stc", piece, server_qkv, preferred_element_type=jnp.float32)
     places = offset + jnp.arange(piece.shape[0], dtype=jnp.int32)
     query_rot = rotate(mixed[:, 0].reshape(-1, heads_here, HEAD_DIM), places).reshape(

time: 513 us -> 473 us (0.922)
  waiting for transfers between devices: 279 us -> 216 us
  local copies, waits for them, and re-layouts: 91.6 us -> 104 us
  starting transfers between devices: 14.5 us -> 22.5 us
    all_gather x1, waiting for transfers between devices: 65.7 us -> 0.01 us  [shards(): lax.all_gather(column_part, 'dp', axis=0, tiled=True)]
    ppermute x0 -> x7, waiting for transfers between devices: none -> 46 us  [the longest x4 46 us: shards(): ppermute(built[-1] if built else normed, axis_name='tensor', perm=all_rows)]
    all_gather x1 -> x0, waiting for transfers between devices: 35.8 us -> none  [shards(): piece = lax.all_gather(normed, 'tensor', axis=0, tiled=True)]
    ppermute x0 -> x7, starting transfers between devices: none -> 8.33 us  [the longest x3 8.32 us: shards(): ppermute(shaped[-1] if shaped else normed, axis_name='tensor', perm=fields)]
    unnamed x35 -> x53, local copies, waits for them, and re-layouts: 30.7 us -> 38.5 us
    all_gather x1, waiting for transfers between devices: 9.96 us -> 2.3 us  [shards(): lax.all_gather(out_cast, 'dp', axis=0, tiled=True)]
    gather x0 -> x1, local copies, waits for them, and re-layouts: none -> 5.36 us  [shards(): q_next = q_next[(jnp.arange(many) - part_now) % many]]
  transfers between devices with their start and end apart: 9 -> 15, of which waited for: 8 -> 10; matrix products, arithmetic and copies ran while one was open for 19% -> 23% of each run, Pallas kernels for 0% -> 0%
where the time goes in v1:
time: 473 us; the launch traced here: 467 us
  waiting for transfers between devices  216 us (46%)
  local copies, waits for them, and re-layouts  104 us (22%)
  other arithmetic  50.9 us (11%)
  matrix products  38.5 us (8%)
  starting transfers between devices  22.5 us (5%)
  blocking collectives  18.9 us (4%)
  between operations  15.7 us (3%)
    reduce_scatter x1, waiting for transfers between devices, shards(): lax.psum_scatter(jnp.dot(attended, server_out, preferred_element_type=jnp...  52.6 us
    ppermute x4, waiting for transfers between devices, shards(): ppermute(built[-1] if built else normed, axis_name='tensor', perm=all_rows)  46 us
    unnamed x53, local copies, waits for them, and re-layouts  38.5 us
    all_to_all x1, waiting for transfers between devices, shards(): lax.all_to_all(trainer_gate.astype(jnp.bfloat16), 'tensor', split_axis=1,...  35.8 us
    reduce_scatter x1, waiting for transfers between devices, shards(): lax.psum_scatter(terms.astype(jnp.bfloat16), 'tensor', scatter_dimension=...  31.4 us
    all_to_all x1, waiting for transfers between devices, shards(): lax.all_to_all(trainer_up.astype(jnp.bfloat16), 'tensor', split_axis=1, c...  24.2 us
    all_to_all x1, waiting for transfers between devices, shards(): lax.all_to_all(trainer_down.astype(jnp.bfloat16), 'tensor', split_axis=1,...  24 us
    all_to_all x1, blocking collectives, shards(): lax.all_to_all(qkv_cast, 'tensor', split_axis=2, concat_axis=0, tiled=True)  18.9 us
  transfers between devices with their start and end apart: 15, of which 10 were waited for; matrix products, arithmetic and copies ran while one was open for 23% of the time, Pallas kernels for 0%

profile of v1, /device:TPU:0, one launch (start us, length us, event | category | flops | bytes accessed | tf_op | source)
XLA Modules:
  0.0 466.8 jit_solution(15358737412848456474)
XLA Ops:
  7.2 2.5 convert_element_type.92
  9.7 2.9 copy.59
  12.6 3.7 reshape.345
  16.3 18.9 %all_to_all.75 = bf16[8,2,27648]{2,1,0:T(2,128)(2,1)} all-to-all(bf16[8,2,27648]{2,1,0:T(2,128)(2,1)} %reshape.345), channel_id=1, replica_groups=mesh['dp'=4,'tensor'=8] {'tensor'}, dimensions={0} | all-to-all | bytes 1769472 | tf_op jit(solution)/shard_map/all_to_all | solution.py:85
  35.2 4.5 reshape.346
  43.2 10.4 %collective-permute-done = bf16[128,2304]{1,0:T(8,128)(2,1)S(1)} collective-permute-done((bf16[128,2304]{1,0:T(8,128)(2,1)}, bf16[128,2304]{1,0:T(8,128)(2,1)S(1)}, u32[]{:S(2)}, u32[]{:S(2)}) %collective-permute-start) | collective-permute-done | bytes 589856 | tf_op jit(solution)/shard_map/ppermute | solution.py:111
  53.6 2.6 collective-permute-start.4
  56.3 13.2 %collective-permute-done.1 = bf16[128,2304]{1,0:T(8,128)(2,1)S(1)} collective-permute-done((bf16[128,2304]{1,0:T(8,128)(2,1)S(1)}, bf16[128,2304]{1,0:T(8,128)(2,1)S(1)}, u32[]{:S(2)}, u32[]{:S(2)}) %collective-permute-start.1) | collective-permute-done | bytes 589856 | tf_op jit(solution)/shard_map/ppermute | solution.py:111
  71.0 2.7 collective-permute-start.5
  73.7 11.3 %collective-permute-done.2 = bf16[128,2304]{1,0:T(8,128)(2,1)} collective-permute-done((bf16[128,2304]{1,0:T(8,128)(2,1)S(1)}, bf16[128,2304]{1,0:T(8,128)(2,1)}, u32[]{:S(2)}, u32[]{:S(2)}) %collective-permute-start.2) | collective-permute-done | bytes 589856 | tf_op jit(solution)/shard_map/ppermute | solution.py:111
  87.4 3.0 collective-permute-start.6
  90.4 11.1 %collective-permute-done.3 = bf16[128,2304]{1,0:T(8,128)(2,1)S(1)} collective-permute-done((bf16[128,2304]{1,0:T(8,128)(2,1)}, bf16[128,2304]{1,0:T(8,128)(2,1)S(1)}, u32[]{:S(2)}, u32[]{:S(2)}) %collective-permute-start.3) | collective-permute-done | bytes 589856 | tf_op jit(solution)/shard_map/ppermute | solution.py:111
  109.6 5.4 %gather_fusion = bf16[8,128,2304]{2,1,0:T(8,128)(2,1)} fusion(bf16[8,128,2304]{2,1,0:T(8,128)(2,1)} %bitcast_dynamic-update-slice_fusion, s32[1024]{0:T(1024)S(1)} %pad_clamp_fusion.1), kind=kCustom, calls=%fused_computation | custom fusion | bytes 9437216 | tf_op jit(solution)/shard_map/gather | solution.py:120
  115.0 2.5 copy.62
  118.4 4.0 fusion.67
  124.4 4.8 %fusion.69 = (f32[4,512]{1,0:T(4,128)S(1)}, f32[4,512,512]{1,2,0:T(8,128)}) fusion(pred[512,512]{0,1:T(8,128)(4,1)S(1)} %copy-done.14, bf16[1024,4,32]{0,2,1:T(8,128)(2,1)S(1)} %get-tuple-element.48, bf16[1024,4,32]{0,2,1:T(8,128)(2,1)S(1)} %get-tuple-element.49, bf16[1024,4,32]{0,2,1:T(8,128)(2,1)} %get-tuple-element.53, ...), kind=kOutput, calls=%fused_computation.128 | convolution fusion | flops 139461120 | bytes 5513216 | tf_op jit(solution)/shard_map/sub | solution.py:48
  129.1 5.4 %fusion.68 = (f32[4,512]{1,0:T(4,128)S(1)}, f32[4,512,1024]{2,1,0:T(8,128)}) fusion(pred[512,1024]{1,0:T(8,128)(4,1)S(1)} %iota_compare_fusion, bf16[1024,4,32]{0,2,1:T(8,128)(2,1)S(1)} %get-tuple-element.52, bf16[1024,4,32]{0,2,1:T(8,128)(2,1)S(1)} %copy-done.15, bf16[1024,4,32]{0,2,1:T(8,128)(2,1)S(1)} %get-tuple-element.49, ...), kind=kOutput, calls=%fused_computation.127 | convolution fusion | flops 278397952 | bytes 9969664 | tf_op jit(solution)/shard_map/sub | solution.py:48
  134.5 2.9 fusion.31
  140.7 2.3 all-gather.6.cloned.1.call-done
  143.0 4.9 %convolution_convert_fusion = bf16[1024,2304]{1,0:T(8,128)(2,1)} fusion(bf16[1024,256]{0,1:T(8,128)(2,1)S(1)} %bitcast.133, bf16[256,2304]{1,0:T(8,128)(2,1)} %all-gather.6.cloned.1.call-done), kind=kOutput, calls=%fused_computation.10 | convolution fusion | flops 1210318848 | bytes 6422528 | tf_op jit(solution)/shard_map/dot_general | solution.py:144
  148.5 52.6 %reduce-scatter.3.cloned.1.call-done = bf16[128,2304]{1,0:T(8,128)(2,1)} async-done(((bf16[1024,2304]{1,0:T(8,128)(2,1)}), bf16[128,2304]{1,0:T(8,128)(2,1)}) %reduce-scatter.3.cloned.1.call-update) | async-done | bytes 589840 | tf_op jit(solution)/shard_map/reduce_scatter | solution.py:143
  204.6 4.9 %convert_element_type.94 = bf16[288,5760]{1,0:T(8,128)(2,1)} convert(f32[288,5760]{1,0:T(8,128)} %param.18) | non-fusion elementwise | flops 1658880 | bytes 9953280 | tf_op jit(solution)/shard_map/convert_element_type | solution.py:73
  209.5 8.6 %all_to_all.59 = bf16[288,8,720]{2,1,0:T(8,128)(2,1)} reshape(bf16[288,5760]{1,0:T(8,128)(2,1)} %convert_element_type.94) | data formatting | bytes 6635520 | tf_op jit(solution)/shard_map/all_to_all | solution.py:72
  218.1 4.5 copy.63
  222.6 4.5 all-to-all-start.1
  227.1 5.0 %convert_element_type.95 = bf16[288,5760]{1,0:T(8,128)(2,1)} convert(f32[288,5760]{1,0:T(8,128)} %param.19) | non-fusion elementwise | flops 1658880 | bytes 9953280 | tf_op jit(solution)/shard_map/convert_element_type | solution.py:76
  232.1 8.5 %all_to_all.63 = bf16[288,8,720]{2,1,0:T(8,128)(2,1)} reshape(bf16[288,5760]{1,0:T(8,128)(2,1)} %convert_element_type.95) | data formatting | bytes 6635520 | tf_op jit(solution)/shard_map/all_to_all | solution.py:75
  240.6 4.5 copy.64
  245.0 35.8 %all-to-all-done.1 = bf16[288,8,720]{2,0,1:T(8,128)(2,1)} async-done(((bf16[288,8,720]{2,0,1:T(8,128)(2,1)}), bf16[288,8,720]{2,0,1:T(8,128)(2,1)}, u32[]{:S(2)}, u32[]{:S(2)}) %all-to-all-start.1) | async-done | bytes 3317792 | tf_op jit(solution)/shard_map/all_to_all | solution.py:72
  280.8 4.5 all-to-all-start.2
  285.3 4.9 %convert_element_type.96 = bf16[288,5760]{1,0:T(8,128)(2,1)} convert(f32[288,5760]{1,0:T(8,128)} %param.20) | non-fusion elementwise | flops 1658880 | bytes 9953280 | tf_op jit(solution)/shard_map/convert_element_type | solution.py:79
  290.3 8.5 %all_to_all.67 = bf16[288,8,720]{2,1,0:T(8,128)(2,1)} reshape(bf16[288,5760]{1,0:T(8,128)(2,1)} %convert_element_type.96) | data formatting | bytes 6635520 | tf_op jit(solution)/shard_map/all_to_all | solution.py:78
  298.7 4.5 copy.65
  303.3 24.2 %all-to-all-done.2 = bf16[288,8,720]{2,0,1:T(8,128)(2,1)} async-done(((bf16[288,8,720]{2,0,1:T(8,128)(2,1)}), bf16[288,8,720]{2,0,1:T(8,128)(2,1)}, u32[]{:S(2)}, u32[]{:S(2)}) %all-to-all-start.2) | async-done | bytes 3317792 | tf_op jit(solution)/shard_map/all_to_all | solution.py:75
  327.4 4.5 all-to-all-start.3
  332.6 4.5 scatter_custom_fusion
  337.2 7.8 %gather_fusion.1 = bf16[512,2304]{1,0:T(8,128)(2,1)S(1)} fusion(bf16[1024,2304]{1,0:T(8,128)(2,1)} %all-gather.8.cloned.1.call-done, s32[1024]{0:T(1024)S(1)} %pad_clamp_fusion), kind=kCustom, calls=%fused_computation.1 | custom fusion | bytes 4720640 | tf_op jit(solution)/shard_map/gather | solution.py:174
  345.0 5.0 %fusion.78 = f32[512,720]{0,1:T(8,128)} fusion(bf16[512,2304]{1,0:T(8,128)(2,1)S(1)} %gather_fusion.1, bf16[2304,720]{1,0:T(8,128)(2,1)} %bitcast.8), kind=kOutput, calls=%fused_computation.129 | convolution fusion | flops 1698693120 | bytes 7151616 | tf_op jit(solution)/shard_map/dot_general | solution.py:175
  350.1 24.0 %all-to-all-done.3 = bf16[288,8,720]{2,0,1:T(8,128)(2,1)} async-done(((bf16[288,8,720]{2,0,1:T(8,128)(2,1)}), bf16[288,8,720]{2,0,1:T(8,128)(2,1)}, u32[]{:S(2)}, u32[]{:S(2)}) %all-to-all-start.3) | async-done | bytes 3317792 | tf_op jit(solution)/shard_map/all_to_all | solution.py:78
  374.0 9.9 %fusion.35 = f32[512,2304]{1,0:T(8,128)} fusion(bf16[2304,720]{1,0:T(8,128)(2,1)} %bitcast.12, f32[512,720]{0,1:T(8,128)} %fusion.78, bf16[512,2304]{1,0:T(8,128)(2,1)S(1)} %gather_fusion.1, bf16[2304,720]{1,0:T(8,128)(2,1)} %bitcast.10), kind=kOutput, calls=%fused_computation.54 | convolution fusion | flops 3399598080 | bytes 15187968 | tf_op jit(solution)/shard_map/dot_general | solution.py:178
  384.0 13.3 %scatter_custom_fusion.1 = f32[1024,2304]{1,0:T(8,128)} fusion(s32[512]{0:T(512)S(1)} %get-tuple-element.57, f32[512,2304]{1,0:T(8,128)} %fusion.35, f32[]{:T(128)} %constant.23.clone.1), kind=kCustom, calls=%fused_computation.11 | custom fusion | flops 1179648 | bytes 9437696 | tf_op jit(solution)/shard_map/scatter-add | solution.py:184
  397.2 6.4 %convert_element_type.117 = bf16[1024,2304]{1,0:T(8,128)(2,1)} convert(f32[1024,2304]{1,0:T(8,128)} %scatter_custom_fusion.1) | non-fusion elementwise | flops 2359296 | bytes 14155776 | tf_op jit(solution)/shard_map/convert_element_type | solution.py:187
  404.3 5.7 %copy.68 = bf16[2304,720]{0,1:T(8,128)(2,1)} copy(bf16[2304,720]{1,0:T(8,128)(2,1)} %bitcast.8) | data formatting | bytes 6635520
  410.0 5.9 %copy.69 = bf16[2304,720]{0,1:T(8,128)(2,1)} copy(bf16[2304,720]{1,0:T(8,128)(2,1)} %bitcast.10) | data formatting | bytes 6635520
  416.0 5.7 %copy.70 = bf16[2304,720]{0,1:T(8,128)(2,1)} copy(bf16[2304,720]{1,0:T(8,128)(2,1)} %bitcast.12) | data formatting | bytes 6635520
  422.9 2.3 copy.71
  425.4 31.4 %reduce-scatter.5.cloned.1.call-done = bf16[128,2304]{1,0:T(8,128)(2,1)} async-done(((bf16[1024,2304]{1,0:T(8,128)(2,1)}), bf16[128,2304]{1,0:T(8,128)(2,1)}) %reduce-scatter.5.cloned.1.call-update) | async-done | bytes 589840 | tf_op jit(solution)/shard_map/reduce_scatter | solution.py:186
  456.8 2.2 fusion.36
  (109 shorter events, 28.4 us)
Async XLA Ops:
  7.2 418.0 %copy-start = (bf16[2304,8]{0,1:T(8,128)(2,1)S(1)}, bf16[2304,8]{0,1:T(8,128)(2,1)}, u32[]{:S(2)}) copy-start(bf16[2304,8]{0,1:T(8,128)(2,1)} %param.23) | copy-start | bytes 110596
  7.2 107.8 %all-gather.4.cloned.1.call-start = ((), (), s32[]{:S(2)}) async-start(), calls=%async_computation.6 | async-start | bytes 4423680 | tf_op jit(solution)/shard_map/all_gather | solution.py:87
  35.2 6.8 %copy-start.1 = (bf16[1,128,2304]{2,1,0:T(8,128)(2,1)S(1)}, bf16[1,128,2304]{2,1,0:T(8,128)(2,1)}, u32[]{:S(2)}) copy-start(bf16[1,128,2304]{2,1,0:T(8,128)(2,1)} %param.12) | copy-start | bytes 1769476
  35.2 7.0 %copy-start.16 = (f32[2304]{0:T(1024)S(1)}, f32[2304]{0:T(1024)}, u32[]{:S(2)}) copy-start(f32[2304]{0:T(1024)} %param.21) | copy-start | bytes 27652
  39.7 29.8 %copy-start.11 = (f32[64,2304]{1,0:T(8,128)S(1)}, f32[64,2304]{1,0:T(8,128)}, u32[]{:S(2)}) copy-start(f32[64,2304]{1,0:T(8,128)} %param.17) | copy-start | bytes 1769476
  41.9 101.1 %all-gather.6.cloned.1.call-start = ((), (), s32[]{:S(2)}) async-start(), calls=%async_computation.7 | async-start | bytes 1474560 | tf_op jit(solution)/shard_map/all_gather | solution.py:88
  43.2 10.4 %collective-permute-start = (bf16[128,2304]{1,0:T(8,128)(2,1)}, bf16[128,2304]{1,0:T(8,128)(2,1)S(1)}, u32[]{:S(2)}, u32[]{:S(2)}) collective-permute-start(bf16[128,2304]{1,0:T(8,128)(2,1)} %fusion.21), channel_id=1, source_target_pairs={{0,1},{1,2},{2,3},{3,4},{4,5},{5,6},{6,7},{7,0},{8,9},{9,10},{10,1... | collective-permute-start | bytes 1769480 | tf_op jit(solution)/shard_map/ppermute | solution.py:111
  53.6 15.8 %collective-permute-start.1 = (bf16[128,2304]{1,0:T(8,128)(2,1)S(1)}, bf16[128,2304]{1,0:T(8,128)(2,1)S(1)}, u32[]{:S(2)}, u32[]{:S(2)}) collective-permute-start(bf16[128,2304]{1,0:T(8,128)(2,1)S(1)} %collective-permute-done), channel_id=1, source_target_pairs={{0,1},{1,2},{2,3},{3,4},{4,5},{5,6},{6,7},{7,0},{8,9},{9,10},{10,1... | collective-permute-start | bytes 1769480 | tf_op jit(solution)/shard_map/ppermute | solution.py:111
  53.6 17.3 %collective-permute-start.4 = (bf16[128,2304]{1,0:T(8,128)(2,1)}, bf16[128,2304]{1,0:T(8,128)(2,1)S(1)}, u32[]{:S(2)}, u32[]{:S(2)}) collective-permute-start(bf16[128,2304]{1,0:T(8,128)(2,1)} %fusion.21), channel_id=1, source_target_pairs={{1,0},{2,1},{3,2},{4,3},{5,4},{6,5},{7,6},{0,7},{9,8},{10,9},{11,1... | collective-permute-start | bytes 1769480 | tf_op jit(solution)/shard_map/ppermute | solution.py:114
  69.4 15.5 %collective-permute-start.2 = (bf16[128,2304]{1,0:T(8,128)(2,1)S(1)}, bf16[128,2304]{1,0:T(8,128)(2,1)}, u32[]{:S(2)}, u32[]{:S(2)}) collective-permute-start(bf16[128,2304]{1,0:T(8,128)(2,1)S(1)} %collective-permute-done.1), channel_id=1, source_target_pairs={{0,1},{1,2},{2,3},{3,4},{4,5},{5,6},{6,7},{7,0},{8,9},{9,10},{10,1... | collective-permute-start | bytes 1769480 | tf_op jit(solution)/shard_map/ppermute | solution.py:111
  70.2 130.9 %reduce-scatter.3.cloned.1.call-start = ((), (), s32[]{:S(2)}) async-start(), calls=%async_computation.8 | async-start | bytes 5308416 | tf_op jit(solution)/shard_map/reduce_scatter | solution.py:143
  71.0 16.4 %collective-permute-start.5 = (bf16[128,2304]{1,0:T(8,128)(2,1)S(1)}, bf16[128,2304]{1,0:T(8,128)(2,1)S(1)}, u32[]{:S(2)}, u32[]{:S(2)}) collective-permute-start(bf16[128,2304]{1,0:T(8,128)(2,1)S(1)} %collective-permute-done.4), channel_id=1, source_target_pairs={{1,0},{2,1},{3,2},{4,3},{5,4},{6,5},{7,6},{0,7},{9,8},{10,9},{11,1... | collective-permute-start | bytes 1769480 | tf_op jit(solution)/shard_map/ppermute | solution.py:114
  85.0 16.5 %collective-permute-start.3 = (bf16[128,2304]{1,0:T(8,128)(2,1)}, bf16[128,2304]{1,0:T(8,128)(2,1)S(1)}, u32[]{:S(2)}, u32[]{:S(2)}) collective-permute-start(bf16[128,2304]{1,0:T(8,128)(2,1)} %collective-permute-done.2), channel_id=1, source_target_pairs={{0,1},{1,2},{2,3},{3,4},{4,5},{5,6},{6,7},{7,0},{8,9},{9,10},{10,1... | collective-permute-start | bytes 1769480 | tf_op jit(solution)/shard_map/ppermute | solution.py:111
  87.4 21.4 %collective-permute-start.6 = (bf16[128,2304]{1,0:T(8,128)(2,1)S(1)}, bf16[128,2304]{1,0:T(8,128)(2,1)S(1)}, u32[]{:S(2)}, u32[]{:S(2)}) collective-permute-start(bf16[128,2304]{1,0:T(8,128)(2,1)S(1)} %collective-permute-done.5), channel_id=1, source_target_pairs={{1,0},{2,1},{3,2},{4,3},{5,4},{6,5},{7,6},{0,7},{9,8},{10,9},{11,1... | collective-permute-start | bytes 1769480 | tf_op jit(solution)/shard_map/ppermute | solution.py:114
  115.0 3.4 copy-start.5
  117.5 4.8 %copy-start.6 = (bf16[8,4,72,3,256]{4,2,1,0,3:T(8,128)(2,1)}, bf16[8,4,72,3,256]{4,2,1,0,3:T(8,128)(2,1)S(1)}, u32[]{:S(2)}) copy-start(bf16[8,4,72,3,256]{4,2,1,0,3:T(8,128)(2,1)S(1)} %copy.62) | copy-start | bytes 10616836
  122.3 0.9 copy-start.12
  122.4 1.0 copy-start.13
  122.4 1.9 copy-start.14
  124.3 4.8 %copy-start.7 = (bf16[1024,4,32]{0,2,1:T(8,128)(2,1)}, bf16[1024,4,32]{0,2,1:T(8,128)(2,1)S(1)}, u32[]{:S(2)}) copy-start(bf16[1024,4,32]{0,2,1:T(8,128)(2,1)S(1)} %get-tuple-element.48) | copy-start | bytes 786436
  124.3 4.8 %copy-start.9 = (bf16[1024,4,32]{0,2,1:T(8,128)(2,1)}, bf16[1024,4,32]{0,2,1:T(8,128)(2,1)S(1)}, u32[]{:S(2)}) copy-start(bf16[1024,4,32]{0,2,1:T(8,128)(2,1)S(1)} %get-tuple-element.49) | copy-start | bytes 786436
  124.3 4.8 %copy-start.15 = (bf16[1024,4,32]{0,2,1:T(8,128)(2,1)S(1)}, bf16[1024,4,32]{0,2,1:T(8,128)(2,1)}, u32[]{:S(2)}) copy-start(bf16[1024,4,32]{0,2,1:T(8,128)(2,1)} %get-tuple-element.53) | copy-start | bytes 786436
  134.5 4.7 %copy-start.19 = (f32[4,512,1024]{2,1,0:T(8,128)S(1)}, f32[4,512,1024]{2,1,0:T(8,128)}, u32[]{:S(2)}) copy-start(f32[4,512,1024]{2,1,0:T(8,128)} %get-tuple-element.63) | copy-start | bytes 25165828
  147.9 54.5 %copy-start.17 = (f32[2304]{0:T(1024)S(1)}, f32[2304]{0:T(1024)}, u32[]{:S(2)}) copy-start(f32[2304]{0:T(1024)} %param.22) | copy-start | bytes 27652
  147.9 189.3 %all-gather.8.cloned.1.call-start = ((), (), s32[]{:S(2)}) async-start(), calls=%async_computation.9 | async-start | bytes 5308416 | tf_op jit(solution)/shard_map/all_gather | solution.py:164
  222.6 58.2 %all-to-all-start.1 = ((bf16[288,8,720]{2,0,1:T(8,128)(2,1)}), bf16[288,8,720]{2,0,1:T(8,128)(2,1)}, u32[]{:S(2)}, u32[]{:S(2)}) async-start(bf16[288,8,720]{2,0,1:T(8,128)(2,1)} %copy.63), calls=%async_computation.1 | async-start | bytes 7077888 | tf_op jit(solution)/shard_map/all_to_all | solution.py:72
  280.8 46.6 %all-to-all-start.2 = ((bf16[288,8,720]{2,0,1:T(8,128)(2,1)}), bf16[288,8,720]{2,0,1:T(8,128)(2,1)}, u32[]{:S(2)}, u32[]{:S(2)}) async-start(bf16[288,8,720]{2,0,1:T(8,128)(2,1)} %copy.64), calls=%async_computation.2 | async-start | bytes 7077888 | tf_op jit(solution)/shard_map/all_to_all | solution.py:75
  303.3 28.7 %copy-start.18 = (s32[1,1024,2]{1,2,0:T(2,128)S(1)}, s32[1,1024,2]{1,2,0:T(2,128)}, u32[]{:S(2)}) copy-start(s32[1,1024,2]{1,2,0:T(2,128)} %param.15) | copy-start | bytes 24580
  327.4 46.6 %all-to-all-start.3 = ((bf16[288,8,720]{2,0,1:T(8,128)(2,1)}), bf16[288,8,720]{2,0,1:T(8,128)(2,1)}, u32[]{:S(2)}, u32[]{:S(2)}) async-start(bf16[288,8,720]{2,0,1:T(8,128)(2,1)} %copy.65), calls=%async_computation.3 | async-start | bytes 7077888 | tf_op jit(solution)/shard_map/all_to_all | solution.py:78
  331.9 124.9 %reduce-scatter.5.cloned.1.call-start = ((), (), s32[]{:S(2)}) async-start(), calls=%async_computation.10 | async-start | bytes 5308416 | tf_op jit(solution)/shard_map/reduce_scatter | solution.py:186
  416.0 5.7 %copy-start.8 = (bf16[1024,4,32]{0,2,1:T(8,128)(2,1)S(1)}, bf16[1024,4,32]{0,2,1:T(8,128)(2,1)}, u32[]{:S(2)}) copy-start(bf16[1024,4,32]{0,2,1:T(8,128)(2,1)} %copy-done.7) | copy-start | bytes 786436
  416.0 5.7 %copy-start.10 = (bf16[1024,4,32]{0,2,1:T(8,128)(2,1)S(1)}, bf16[1024,4,32]{0,2,1:T(8,128)(2,1)}, u32[]{:S(2)}) copy-start(bf16[1024,4,32]{0,2,1:T(8,128)(2,1)} %copy-done.9) | copy-start | bytes 786436
  421.7 3.4 copy-start.2
  421.7 35.1 %copy-start.3 = (bf16[128,2304]{1,0:T(8,128)(2,1)S(1)}, bf16[128,2304]{1,0:T(8,128)(2,1)}, u32[]{:S(2)}) copy-start(bf16[128,2304]{1,0:T(8,128)(2,1)} %reduce-scatter.3.cloned.1.call-done) | copy-start | bytes 1769476
  421.8 37.3 %copy-start.4 = (bf16[256,2304]{1,0:T(8,128)(2,1)S(1)}, bf16[256,2304]{1,0:T(8,128)(2,1)}, u32[]{:S(2)}) copy-start(bf16[256,2304]{1,0:T(8,128)(2,1)} %all-gather.6.cloned.1.call-done) | copy-start | bytes 3538948
Sparse Core Ops, SparseCore 0:
  42.0 69.7 all-gather.3
  113.9 29.0 all-gather.5
  148.0 52.9 reduce-scatter.2
  204.7 60.3 all-gather.7
  403.8 53.0 reduce-scatter.4
